TPU v7x, 256 devices: a whole 4x4x8 slice. The times are simulated.
256 devices in a mesh: expert: 64 (over y, z, core), hidden: 4 (over x).
Axes of the slice: x: 4, y: 4, z: 8, core: 2. Of those that a mesh axis runs over, the one named last changes fastest.
Arguments:
- tokens: bfloat16 [8192, 4096], P('expert', 'hidden'), may hold values from -6 to 6
- routes: int32 [8192, 8], P('expert'), may hold values from 0 to 63, all different within a row; in each aligned block of 128 rows (0 to 127, 128 to 255, ...) at most 24 rows name the same one
- route_gates: float32 [8192, 8], P('expert'), may hold values from 0.03 to 0.3
- loss_weights: float32 [8192], P('expert'), may hold values from 0.25 to 4
- damping: float32 [1], replicated, may hold values from 1 to 16
- w_gate: bfloat16 [64, 4096, 768], P('expert', None, 'hidden'), may hold values from -0.09375 to 0.09375
- w_up: bfloat16 [64, 4096, 768], P('expert', None, 'hidden'), may hold values from -0.09375 to 0.09375
- direction: bfloat16 [64, 768, 4096], P('expert', 'hidden'), may hold values from -6 to 6
- residual: bfloat16 [64, 768, 4096], P('expert', 'hidden'), may hold values from -6 to 6
Outputs:
- solution_step: bfloat16 [64, 768, 4096], P('expert', 'hidden')
- new_residual: bfloat16 [64, 768, 4096], P('expert', 'hidden')
- new_direction: bfloat16 [64, 768, 4096], P('expert', 'hidden')
Inputs may be any that keep to these rules, and one draw needn't show every extreme that they name: `routes`: each token names 8 different experts. Among the tokens of one index of expert (aligned blocks of 128 rows) no expert is named more than 24 times, and in every draw some block names some expert exactly 24 times.
All inputs are finite; a program needn't handle non-finite values.
Results may differ from a plain program's by a relative error of at most 0.011.
Values may be sent and summed in bfloat16 or wider, within the bound.
A program may use at most 128 MiB of HBM per device.

v0:
```python
import jax
import jax.numpy as jnp
from jax import lax
from jax.sharding import PartitionSpec as P


def per_device(
    tokens, routes, route_gates, loss_weights, damping, w_gate, w_up, direction, residual
):
    experts = lax.axis_size("expert")
    tok_rows, top_routes = routes.shape
    capacity = min(tok_rows, 3 * tok_rows * top_routes // (2 * experts))
    route_count = tok_rows * top_routes
    slot_count = experts * capacity
    flat_routes = routes.reshape(-1)
    one_hot = (flat_routes[:, None] == jnp.arange(experts, dtype=jnp.int32)[None, :]).astype(
        jnp.int32
    )
    earlier = jnp.cumsum(one_hot, axis=0) - one_hot
    position = jnp.sum(earlier * one_hot, axis=1)
    slot_of_route = flat_routes * capacity + position
    route_of_slot = (
        jnp.full((slot_count,), route_count, jnp.int32)
        .at[slot_of_route]
        .set(jnp.arange(route_count, dtype=jnp.int32))
    )
    filled = route_of_slot < route_count
    safe_route = jnp.minimum(route_of_slot, route_count - 1)
    token_of_slot = safe_route // top_routes

    def pack_rows(source_rows, index):
        picked = source_rows[index]
        return jnp.where(filled[:, None], picked, jnp.zeros((), picked.dtype)).reshape(
            experts, capacity, -1
        )

    gate_local = w_gate[0]
    up_local = w_up[0]
    whole_tokens = lax.all_gather(tokens, "hidden", axis=1, tiled=True)
    send_rows = pack_rows(whole_tokens, token_of_slot)
    arrived = lax.all_to_all(send_rows, "expert", split_axis=0, concat_axis=0, tiled=True).reshape(
        slot_count, -1
    )
    pre_gate = jnp.dot(arrived, gate_local, preferred_element_type=jnp.float32)
    pre_up = jnp.dot(arrived, up_local, preferred_element_type=jnp.float32)
    hidden = (jax.nn.silu(pre_gate) * pre_up).astype(jnp.bfloat16)
    hidden_full = lax.all_gather(hidden, "hidden", axis=1, tiled=True)
    search_cols = lax.all_to_all(direction[0], "hidden", split_axis=1, concat_axis=0, tiled=True)
    tangent = jnp.dot(hidden_full, search_cols, preferred_element_type=jnp.float32).astype(
        jnp.bfloat16
    )
    returned = lax.all_to_all(
        tangent.reshape(experts, capacity, -1), "expert", split_axis=0, concat_axis=0, tiled=True
    ).reshape(slot_count, -1)
    per_route = returned[slot_of_route].reshape(tok_rows, top_routes, -1)
    combined = jnp.einsum("tjd,tj->td", per_route.astype(jnp.float32), route_gates)
    scaled = combined * loss_weights[:, None]
    cotangent = (
        (route_gates[:, :, None] * scaled[:, None, :]).astype(jnp.bfloat16).reshape(route_count, -1)
    )
    send_back = pack_rows(cotangent, safe_route)
    back_rows = lax.all_to_all(
        send_back, "expert", split_axis=0, concat_axis=0, tiled=True
    ).reshape(slot_count, -1)
    curvature_cols = lax.dot_general(
        hidden_full, back_rows, (((0,), (0,)), ((), ())), preferred_element_type=jnp.float32
    )
    curvature = lax.all_to_all(curvature_cols, "hidden", split_axis=0, concat_axis=1, tiled=True)
    search = direction[0].astype(jnp.float32)
    resid = residual[0].astype(jnp.float32)
    image = search + curvature / damping[0]
    pq_total, rr_total = lax.psum(
        (jnp.sum(search * image), jnp.sum(resid * resid)), ("expert", "hidden")
    )
    alpha_step = rr_total / pq_total
    updated = resid - alpha_step * image
    rr_new = lax.psum(jnp.sum(updated * updated), ("expert", "hidden"))
    beta_ratio = rr_new / rr_total
    solution_step = (alpha_step * search).astype(jnp.bfloat16)[None]
    new_residual = updated.astype(jnp.bfloat16)[None]
    new_direction = (updated + beta_ratio * search).astype(jnp.bfloat16)[None]
    return (solution_step, new_residual, new_direction)


def solution(mesh):
    return jax.shard_map(
        per_device,
        mesh=mesh,
        in_specs=(
            P("expert", "hidden"),
            P("expert", None),
            P("expert", None),
            P("expert"),
            P(),
            P("expert", None, "hidden"),
            P("expert", None, "hidden"),
            P("expert", "hidden", None),
            P("expert", "hidden", None),
        ),
        out_specs=(
            P("expert", "hidden", None),
            P("expert", "hidden", None),
            P("expert", "hidden", None),
        ),
        check_vma=False,
    )
```

profile of v0, /device:TPU:1, one launch (start us, length us, event | category | flops | bytes accessed | tf_op | source)
XLA Modules:
  0.0 834.8 jit_solution(10602769745563700831)
XLA Ops:
  9.0 18.0 %reduce-window.6 = s32[64,8,128]{2,1,0:T(8,128)S(1)} reduce-window(s32[64,8,128]{2,1,0:T(8,128)S(1)} %fusion.25, s32[]{:T(128)} %constant.30.clone.1), window={size=1x1x128 pad=0_0x0_0x127_0}, to_apply=%region_2.3 | reduce-window | flops 8323072 | bytes 524292 | tf_op jit(solution)/shard_map/reduce-window
  28.5 4.3 scatter_custom_fusion
  33.0 5.2 all-gather.3.cloned.1.call-done
  38.2 23.4 %gather_fusion = bf16[1536,4096]{1,0:T(8,128)(2,1)} fusion(bf16[128,4096]{1,0:T(8,128)(2,1)} %all-gather.3.cloned.1.call-done, s32[2048]{0:T(1024)S(1)} %pad_clamp_fusion.1), kind=kCustom, calls=%fused_computation | custom fusion | bytes 25171968 | tf_op jit(solution)/shard_map/gather | solution.py:32
  61.6 6.3 broadcast_select_fusion
  67.9 288.5 %all_to_all.44 = bf16[64,24,4096]{2,1,0:T(8,128)(2,1)S(1)} all-to-all(bf16[64,24,4096]{2,1,0:T(8,128)(2,1)S(1)} %broadcast_select_fusion), channel_id=1, replica_groups=mesh['expert'=64,'hidden'=4] {'expert'}, dimensions={0} | all-to-all | bytes 25165824 | tf_op jit(solution)/shard_map/all_to_all | solution.py:41
  356.4 4.3 fusion.17
  360.7 5.2 fusion.13
  365.9 2.4 all_to_all.32
  368.3 1.9 copy.35
  370.2 39.1 %all_to_all.45 = bf16[192,4,1024]{2,0,1:T(8,128)(2,1)} all-to-all(bf16[192,4,1024]{2,0,1:T(8,128)(2,1)S(1)} %copy.35), channel_id=1, replica_groups=mesh['expert'=64,'hidden'=4] {'hidden'}, dimensions={1} | all-to-all | bytes 3145728 | tf_op jit(solution)/shard_map/all_to_all | solution.py:48
  409.3 4.1 all-gather.5.cloned.1.call-done
  413.4 6.5 convolution_convert_fusion
  419.9 6.0 all-to-all-start.2
  426.4 73.0 %all-to-all-done.2 = bf16[64,24,1024]{2,1,0:T(8,128)(2,1)} async-done(((bf16[64,24,1024]{2,1,0:T(8,128)(2,1)}), bf16[64,24,1024]{2,1,0:T(8,128)(2,1)}, u32[]{:S(2)}, u32[]{:S(2)}) %all-to-all-start.2) | async-done | bytes 3145760 | tf_op jit(solution)/shard_map/all_to_all | solution.py:52
  499.4 8.4 %gather_fusion.1 = bf16[1024,1024]{1,0:T(8,128)(2,1)} fusion(bf16[1536,1024]{1,0:T(8,128)(2,1)} %bitcast.15, s32[1024]{0:T(1024)S(1)} %broadcast_clamp_fusion), kind=kCustom, calls=%fused_computation.1 | custom fusion | bytes 4198400 | tf_op jit(solution)/shard_map/gather | solution.py:55
  507.7 2.3 fusion.14
  510.2 1.7 fusion
  511.9 9.7 %gather_fusion.2 = bf16[1536,1024]{1,0:T(8,128)(2,1)} fusion(bf16[1024,1024]{1,0:T(8,128)(2,1)} %fusion, s32[2048]{0:T(1024)S(1)} %pad_clamp_fusion), kind=kCustom, calls=%fused_computation.2 | custom fusion | bytes 6297600 | tf_op jit(solution)/shard_map/gather | solution.py:32
  521.5 2.1 broadcast_select_fusion.1
  523.6 79.1 %all_to_all.46 = bf16[64,24,1024]{2,1,0:T(8,128)(2,1)S(1)} all-to-all(bf16[64,24,1024]{2,1,0:T(8,128)(2,1)S(1)} %broadcast_select_fusion.1), channel_id=1, replica_groups=mesh['expert'=64,'hidden'=4] {'expert'}, dimensions={0} | all-to-all | bytes 6291456 | tf_op jit(solution)/shard_map/all_to_all | solution.py:62
  602.8 4.3 fusion.30
  607.0 4.6 all-to-all-start.4
  612.3 37.1 %all-to-all-done.4 = f32[4,192,1024]{2,1,0:T(8,128)} async-done(((f32[4,192,1024]{2,1,0:T(8,128)}), f32[4,192,1024]{2,1,0:T(8,128)}, u32[]{:S(2)}, u32[]{:S(2)}) %all-to-all-start.4) | async-done | bytes 3145760 | tf_op jit(solution)/shard_map/all_to_all | solution.py:68
  649.4 4.6 fusion.21
  655.6 1.6 fusion.5
  657.2 74.2 %all-reduce = (f32[]{:T(128)}, f32[]{:T(128)}) all-reduce(f32[]{:T(128)} %get-tuple-element.12, f32[]{:T(128)} %get-tuple-element.13), channel_id=1, replica_groups=mesh['expert'=64,'hidden'=4] {'expert','hidden'}, use_global_device_ids=true, to_apply=%region_1.2 | all-reduce | flops 2 | bytes 16 | tf_op jit(solution)/shard_map/psum | solution.py:72
  732.7 3.3 fusion.7
  736.0 74.3 %psum.23 = f32[]{:T(128)} all-reduce(f32[]{:T(128)} %fusion.7), channel_id=1, replica_groups=mesh['expert'=64,'hidden'=4] {'expert','hidden'}, use_global_device_ids=true, to_apply=%region_9.10 | all-reduce | flops 1 | bytes 8 | tf_op jit(solution)/shard_map/psum | solution.py:77
  811.6 5.6 copy.36
  817.3 5.4 div.56
  822.6 5.3 fusion.12
  (49 shorter events, 5.5 us)
Async XLA Ops:
  7.2 349.3 %copy-start = (bf16[1,4096,192]{1,2,0:T(8,128)(2,1)S(1)}, bf16[1,4096,192]{1,2,0:T(8,128)(2,1)}, u32[]{:S(2)}) copy-start(bf16[1,4096,192]{1,2,0:T(8,128)(2,1)} %param.14) | copy-start | bytes 4718596
  7.2 31.0 %all-gather.3.cloned.1.call-start = ((), (), s32[]{:S(2)}) async-start(), calls=%async_computation.5 | async-start | bytes 1310720 | tf_op jit(solution)/shard_map/all_gather | solution.py:39
  7.9 405.5 %all-gather.5.cloned.1.call-start = ((), (), s32[]{:S(2)}) async-start(), calls=%async_computation.6 | async-start | bytes 2949120 | tf_op jit(solution)/shard_map/all_gather | solution.py:47
  356.4 4.3 copy-start.8
  360.7 5.2 copy-start.3
  419.9 6.1 copy-start.5
  419.9 79.4 %all-to-all-start.2 = ((bf16[64,24,1024]{2,1,0:T(8,128)(2,1)}), bf16[64,24,1024]{2,1,0:T(8,128)(2,1)}, u32[]{:S(2)}, u32[]{:S(2)}) async-start(bf16[64,24,1024]{2,1,0:T(8,128)(2,1)} %bitcast.94), calls=%async_computation.2 | async-start | bytes 6291456 | tf_op jit(solution)/shard_map/all_to_all | solution.py:52
  499.4 10.6 %copy-start.6 = (f32[128]{0:T(128)S(1)}, f32[128]{0:T(128)}, u32[]{:S(2)}) copy-start(f32[128]{0:T(128)} %param.12) | copy-start | bytes 1540
  523.6 79.2 %copy-start.7 = (bf16[1536,768]{0,1:T(8,128)(2,1)S(1)}, bf16[1536,768]{0,1:T(8,128)(2,1)}, u32[]{:S(2)}) copy-start(bf16[1536,768]{0,1:T(8,128)(2,1)} %all-gather.5.cloned.1.call-done) | copy-start | bytes 7077892
  607.0 42.4 %all-to-all-start.4 = ((f32[4,192,1024]{2,1,0:T(8,128)}), f32[4,192,1024]{2,1,0:T(8,128)}, u32[]{:S(2)}, u32[]{:S(2)}) async-start(f32[4,192,1024]{2,1,0:T(8,128)} %fusion.30), calls=%async_computation.4 | async-start | bytes 6291456 | tf_op jit(solution)/shard_map/all_to_all | solution.py:68
  654.0 1.6 copy-start.4
  654.4 2.7 copy-start.2
  817.3 10.7 %copy-start.1 = (bf16[1,4096,192]{1,2,0:T(8,128)(2,1)S(1)}, bf16[1,4096,192]{1,2,0:T(8,128)(2,1)}, u32[]{:S(2)}) copy-start(bf16[1,4096,192]{1,2,0:T(8,128)(2,1)} %param.14) | copy-start | bytes 4718596
Sparse Core Ops, SparseCore 0:
  9.8 28.3 all-gather.2
  366.1 47.3 all-gather.4
where the time goes:
time: 836 us; the launch traced here: 835 us
  blocking collectives  555 us (66%)
  waiting for transfers between devices  120 us (14%)
  local copies, waits for them, and re-layouts  64.5 us (8%)
  other arithmetic  44 us (5%)
  matrix products  22.5 us (3%)
  between operations  17.6 us (2%)
  starting transfers between devices  10.8 us (1%)
    all_to_all x1, blocking collectives, per_device(): lax.all_to_all(send_rows, 'expert', split_axis=0, concat_axis=0, tiled=True)  289 us
    all_to_all x1, blocking collectives, per_device(): lax.all_to_all(send_back, 'expert', split_axis=0, concat_axis=0, tiled=True)  79.1 us
    psum x1, blocking collectives, per_device(): rr_new = lax.psum(jnp.sum(updated * updated), ('expert', 'hidden'))  74.3 us
    psum x1, blocking collectives, per_device(): lax.psum((jnp.sum(search * image), jnp.sum(resid * resid)), ('expert', 'h...  74.2 us
    all_to_all x1, waiting for transfers between devices, per_device(): lax.all_to_all(tangent.reshape(experts, capacity, -1), 'expert', split_ax...  73 us
    all_to_all x1, blocking collectives, per_device(): lax.all_to_all(direction[0], 'hidden', split_axis=1, concat_axis=0, tiled...  39.1 us
    all_to_all x1, waiting for transfers between devices, per_device(): lax.all_to_all(curvature_cols, 'hidden', split_axis=0, concat_axis=1, til...  37.1 us
    gather x2, local copies, waits for them, and re-layouts, pack_rows(): picked = source_rows[index]  33 us
  transfers between devices with their start and end apart: 4, of which 4 were waited for; matrix products, arithmetic and copies ran while one was open for 3% of the time, Pallas kernels for 0%

commit v1 on v0

--- a/solution.py
+++ b/solution.py
@@ -69,8 +69,13 @@
     search = direction[0].astype(jnp.float32)
     resid = residual[0].astype(jnp.float32)
     image = search + curvature / damping[0]
-    pq_total, rr_total = lax.psum(
-        (jnp.sum(search * image), jnp.sum(resid * resid)), ("expert", "hidden")
+
+    def pack_ports(arr_in, lane_axis, group_axis):
+        formed = lax.psum(arr_in, lane_axis)
+        return lax.psum(formed, group_axis)
+
+    pq_total, rr_total = pack_ports(
+        (jnp.sum(search * image), jnp.sum(resid * resid)), lane_axis="hidden", group_axis="expert"
     )
     alpha_step = rr_total / pq_total
     updated = resid - alpha_step * image

time: 836 us -> 894 us (1.069)
  blocking collectives: 555 us -> 614 us
    psum x1 -> x2, blocking collectives: 74.2 us -> 134 us  [the longest x1 127 us: pack_ports(): return lax.psum(formed, group_axis)]
where the time goes in v1:
time: 894 us; the launch traced here: 893 us
  blocking collectives  614 us (69%)
  waiting for transfers between devices  120 us (13%)
  local copies, waits for them, and re-layouts  64.5 us (7%)
  other arithmetic  44 us (5%)
  matrix products  22.5 us (3%)
  between operations  17.6 us (2%)
  starting transfers between devices  10.8 us (1%)
    all_to_all x1, blocking collectives, per_device(): lax.all_to_all(send_rows, 'expert', split_axis=0, concat_axis=0, tiled=True)  289 us
    psum x1, blocking collectives, pack_ports(): return lax.psum(formed, group_axis)  127 us
    all_to_all x1, blocking collectives, per_device(): lax.all_to_all(send_back, 'expert', split_axis=0, concat_axis=0, tiled=True)  79.1 us
    all_to_all x1, waiting for transfers between devices, per_device(): lax.all_to_all(tangent.reshape(experts, capacity, -1), 'expert', split_ax...  73 us
    psum x1, blocking collectives, per_device(): rr_new = lax.psum(jnp.sum(updated * updated), ('expert', 'hidden'))  72.8 us
    all_to_all x1, blocking collectives, per_device(): lax.all_to_all(direction[0], 'hidden', split_axis=1, concat_axis=0, tiled...  39.1 us
    all_to_all x1, waiting for transfers between devices, per_device(): lax.all_to_all(curvature_cols, 'hidden', split_axis=0, concat_axis=1, til...  37.1 us
    gather x2, local copies, waits for them, and re-layouts, pack_rows(): picked = source_rows[index]  33 us
  transfers between devices with their start and end apart: 4, of which 4 were waited for; matrix products, arithmetic and copies ran while one was open for 3% of the time, Pallas kernels for 0%

profile of v1, /device:TPU:1, one launch (start us, length us, event | category | flops | bytes accessed | tf_op | source)
XLA Modules:
  0.0 893.4 jit_solution(12705190566117615908)
XLA Ops:
  9.0 18.0 %reduce-window.6 = s32[64,8,128]{2,1,0:T(8,128)S(1)} reduce-window(s32[64,8,128]{2,1,0:T(8,128)S(1)} %fusion.25, s32[]{:T(128)} %constant.30.clone.1), window={size=1x1x128 pad=0_0x0_0x127_0}, to_apply=%region_3.4 | reduce-window | flops 8323072 | bytes 524292 | tf_op jit(solution)/shard_map/reduce-window
  28.5 4.3 scatter_custom_fusion
  33.0 5.2 all-gather.3.cloned.1.call-done
  38.2 23.4 %gather_fusion = bf16[1536,4096]{1,0:T(8,128)(2,1)} fusion(bf16[128,4096]{1,0:T(8,128)(2,1)} %all-gather.3.cloned.1.call-done, s32[2048]{0:T(1024)S(1)} %pad_clamp_fusion.1), kind=kCustom, calls=%fused_computation | custom fusion | bytes 25171968 | tf_op jit(solution)/shard_map/gather | solution.py:32
  61.6 6.3 broadcast_select_fusion
  67.9 288.5 %all_to_all.44 = bf16[64,24,4096]{2,1,0:T(8,128)(2,1)S(1)} all-to-all(bf16[64,24,4096]{2,1,0:T(8,128)(2,1)S(1)} %broadcast_select_fusion), channel_id=1, replica_groups=mesh['expert'=64,'hidden'=4] {'expert'}, dimensions={0} | all-to-all | bytes 25165824 | tf_op jit(solution)/shard_map/all_to_all | solution.py:41
  356.4 4.3 fusion.17
  360.7 5.2 fusion.13
  365.9 2.4 all_to_all.32
  368.3 1.9 copy.35
  370.2 39.1 %all_to_all.45 = bf16[192,4,1024]{2,0,1:T(8,128)(2,1)} all-to-all(bf16[192,4,1024]{2,0,1:T(8,128)(2,1)S(1)} %copy.35), channel_id=1, replica_groups=mesh['expert'=64,'hidden'=4] {'hidden'}, dimensions={1} | all-to-all | bytes 3145728 | tf_op jit(solution)/shard_map/all_to_all | solution.py:48
  409.3 4.1 all-gather.5.cloned.1.call-done
  413.4 6.5 convolution_convert_fusion
  419.9 6.0 all-to-all-start.2
  426.4 73.0 %all-to-all-done.2 = bf16[64,24,1024]{2,1,0:T(8,128)(2,1)} async-done(((bf16[64,24,1024]{2,1,0:T(8,128)(2,1)}), bf16[64,24,1024]{2,1,0:T(8,128)(2,1)}, u32[]{:S(2)}, u32[]{:S(2)}) %all-to-all-start.2) | async-done | bytes 3145760 | tf_op jit(solution)/shard_map/all_to_all | solution.py:52
  499.4 8.4 gather_fusion.1
  507.7 2.3 fusion.14
  510.2 1.7 fusion
  511.9 9.7 %gather_fusion.2 = bf16[1536,1024]{1,0:T(8,128)(2,1)} fusion(bf16[1024,1024]{1,0:T(8,128)(2,1)} %fusion, s32[2048]{0:T(1024)S(1)} %pad_clamp_fusion), kind=kCustom, calls=%fused_computation.2 | custom fusion | bytes 6297600 | tf_op jit(solution)/shard_map/gather | solution.py:32
  521.5 2.1 broadcast_select_fusion.1
  523.6 79.1 %all_to_all.46 = bf16[64,24,1024]{2,1,0:T(8,128)(2,1)S(1)} all-to-all(bf16[64,24,1024]{2,1,0:T(8,128)(2,1)S(1)} %broadcast_select_fusion.1), channel_id=1, replica_groups=mesh['expert'=64,'hidden'=4] {'expert'}, dimensions={0} | all-to-all | bytes 6291456 | tf_op jit(solution)/shard_map/all_to_all | solution.py:62
  602.8 4.3 fusion.30
  607.0 4.6 all-to-all-start.4
  612.3 37.1 %all-to-all-done.4 = f32[4,192,1024]{2,1,0:T(8,128)} async-done(((f32[4,192,1024]{2,1,0:T(8,128)}), f32[4,192,1024]{2,1,0:T(8,128)}, u32[]{:S(2)}, u32[]{:S(2)}) %all-to-all-start.4) | async-done | bytes 3145760 | tf_op jit(solution)/shard_map/all_to_all | solution.py:68
  649.4 4.6 fusion.21
  657.2 7.5 all-reduce.1
  664.6 126.9 %all-reduce = (f32[]{:T(128)}, f32[]{:T(128)}) all-reduce(f32[]{:T(128)} %get-tuple-element.5, f32[]{:T(128)} %get-tuple-element.6), channel_id=1, replica_groups=mesh['expert'=64,'hidden'=4] {'expert'}, use_global_device_ids=true, to_apply=%region_2.3 | all-reduce | flops 2 | bytes 16 | tf_op jit(solution)/shard_map/psum | solution.py:75
  792.9 3.3 fusion.7
  796.2 72.8 %psum.39 = f32[]{:T(128)} all-reduce(f32[]{:T(128)} %fusion.7), channel_id=1, replica_groups=mesh['expert'=64,'hidden'=4] {'expert','hidden'}, use_global_device_ids=true, to_apply=%region_11.12 | all-reduce | flops 1 | bytes 8 | tf_op jit(solution)/shard_map/psum | solution.py:82
  870.3 5.6 copy.36
  875.9 5.4 div.56
  881.3 5.3 fusion.12
  (50 shorter events, 7.0 us)
Async XLA Ops:
  7.2 349.3 %copy-start = (bf16[1,4096,192]{1,2,0:T(8,128)(2,1)S(1)}, bf16[1,4096,192]{1,2,0:T(8,128)(2,1)}, u32[]{:S(2)}) copy-start(bf16[1,4096,192]{1,2,0:T(8,128)(2,1)} %param.14) | copy-start | bytes 4718596
  7.2 31.0 %all-gather.3.cloned.1.call-start = ((), (), s32[]{:S(2)}) async-start(), calls=%async_computation.5 | async-start | bytes 1310720 | tf_op jit(solution)/shard_map/all_gather | solution.py:39
  7.9 405.5 %all-gather.5.cloned.1.call-start = ((), (), s32[]{:S(2)}) async-start(), calls=%async_computation.6 | async-start | bytes 2949120 | tf_op jit(solution)/shard_map/all_gather | solution.py:47
  356.4 4.3 copy-start.8
  360.7 5.2 copy-start.3
  419.9 6.1 copy-start.5
  419.9 79.4 %all-to-all-start.2 = ((bf16[64,24,1024]{2,1,0:T(8,128)(2,1)}), bf16[64,24,1024]{2,1,0:T(8,128)(2,1)}, u32[]{:S(2)}, u32[]{:S(2)}) async-start(bf16[64,24,1024]{2,1,0:T(8,128)(2,1)} %bitcast.94), calls=%async_computation.2 | async-start | bytes 6291456 | tf_op jit(solution)/shard_map/all_to_all | solution.py:52
  499.4 10.6 %copy-start.6 = (f32[128]{0:T(128)S(1)}, f32[128]{0:T(128)}, u32[]{:S(2)}) copy-start(f32[128]{0:T(128)} %param.12) | copy-start | bytes 1540
  523.6 79.2 %copy-start.7 = (bf16[1536,768]{0,1:T(8,128)(2,1)S(1)}, bf16[1536,768]{0,1:T(8,128)(2,1)}, u32[]{:S(2)}) copy-start(bf16[1536,768]{0,1:T(8,128)(2,1)} %all-gather.5.cloned.1.call-done) | copy-start | bytes 7077892
  607.0 42.4 %all-to-all-start.4 = ((f32[4,192,1024]{2,1,0:T(8,128)}), f32[4,192,1024]{2,1,0:T(8,128)}, u32[]{:S(2)}, u32[]{:S(2)}) async-start(f32[4,192,1024]{2,1,0:T(8,128)} %fusion.30), calls=%async_computation.4 | async-start | bytes 6291456 | tf_op jit(solution)/shard_map/all_to_all | solution.py:68
  654.0 1.6 copy-start.4
  654.4 2.7 copy-start.2
  875.9 10.7 %copy-start.1 = (bf16[1,4096,192]{1,2,0:T(8,128)(2,1)S(1)}, bf16[1,4096,192]{1,2,0:T(8,128)(2,1)}, u32[]{:S(2)}) copy-start(bf16[1,4096,192]{1,2,0:T(8,128)(2,1)} %param.14) | copy-start | bytes 4718596
Sparse Core Ops, SparseCore 0:
  9.8 28.3 all-gather.2
  366.1 47.3 all-gather.4
